TPU v7x, 32 devices: a whole 2x2x4 slice. The times are simulated.
32 devices in a mesh: rep: 2 (over y), shard: 16 (over z, x, core).
Axes of the slice: x: 2, y: 2, z: 4, core: 2. Of those that a mesh axis runs over, the one named last changes fastest.
Arguments:
- images: bfloat16 [32, 14, 14, 512], P(('rep', 'shard')), may hold values from -6 to 6
- cotangent: bfloat16 [32, 14, 14, 512], P(('rep', 'shard')), may hold values from -6 to 6
- regions: int32 [32, 14, 14], P(('rep', 'shard')), may hold values from 0 to 8, as said below
- w_qkv: bfloat16 [2, 512, 1536], P(None, 'shard'), may hold values from -0.25 to 0.25
- w_proj: bfloat16 [2, 512, 512], P(None, 'shard'), may hold values from -0.75 to 0.75
- w_fc1: bfloat16 [2, 512, 2048], P(None, 'shard'), may hold values from -0.25 to 0.25
- w_fc2: bfloat16 [2, 2048, 512], P(None, 'shard'), may hold values from -0.125 to 0.125
- norm_gains: bfloat16 [2, 2, 512], P(None, None, 'shard'), may hold values from 0.5 to 1.5
- norm_shifts: bfloat16 [2, 2, 512], P(None, None, 'shard'), may hold values from -1.1953125 to 1.1953125
- branch_biases: bfloat16 [2, 4, 512], P(None, None, 'shard'), may hold values from -1.1953125 to 1.1953125
- fc1_bias: bfloat16 [2, 2048], P(None, 'shard'), may hold values from -1.1953125 to 1.1953125
- rel_table: bfloat16 [2, 169, 16], replicated, may hold values from -6 to 6
Outputs:
- images_out: bfloat16 [32, 14, 14, 512], P(('rep', 'shard'))
- images_grad: float32 [32, 14, 14, 512], P(('rep', 'shard'))
- grad_w_qkv: float32 [2, 512, 1536], P(None, 'shard')
- grad_w_proj: float32 [2, 512, 512], P(None, 'shard')
- grad_w_fc1: float32 [2, 512, 2048], P(None, 'shard')
- grad_w_fc2: float32 [2, 2048, 512], P(None, 'shard')
- grad_norm_gains: float32 [2, 2, 512], P(None, None, 'shard')
- grad_norm_shifts: float32 [2, 2, 512], P(None, None, 'shard')
- grad_branch_biases: float32 [2, 4, 512], P(None, None, 'shard')
- grad_fc1_bias: float32 [2, 2048], P(None, 'shard')
- grad_rel_table: float32 [2, 169, 16], replicated
Inputs may be any that keep to these rules, and one draw needn't show every extreme that they name: `regions`: in each image the ids are 3 * (row band) + (column band), the rows and the columns each cut into three bands of consecutive positions.
All inputs are finite; a program needn't handle non-finite values.
Results may differ from a plain program's by a relative error of at most 0.023.
Values may be sent and summed in bfloat16 or wider, within the bound.
A program may use at most 128 MiB of HBM per device.

v0:
```python
import jax
import jax.numpy as jnp
from jax import lax
from jax.sharding import PartitionSpec as P

SIDE = 14
WIN = 7
SHIFT = 3
eps = 1e-05
highest = lax.Precision.HIGHEST
inv_root_two = 0.7071067811865476
inv_root_two_pi = 0.3989422804014327


def layer_norm(values, norm_gain, norm_shift):
    row_mean = jnp.mean(values, axis=-1, keepdims=True)
    centred = values - row_mean
    row_var = jnp.mean(centred * centred, axis=-1, keepdims=True)
    return centred * lax.rsqrt(row_var + eps) * norm_gain + norm_shift


def times_transposed(left, right):
    return lax.dot_general(
        left, right, (((1,), (1,)), ((), ())), preferred_element_type=jnp.float32
    )


def transposed_times(left, right):
    return lax.dot_general(
        left, right, (((0,), (0,)), ((), ())), preferred_element_type=jnp.float32
    )


def gelu_slope(pre_act):
    return 0.5 * (1.0 + lax.erf(pre_act * inv_root_two)) + pre_act * inv_root_two_pi * jnp.exp(
        -0.5 * pre_act * pre_act
    )


def to_windows(grid_data):
    image_count = grid_data.shape[0]
    per_side = SIDE // WIN
    trailing = grid_data.shape[3:]
    blocks = grid_data.reshape((image_count, per_side, WIN, per_side, WIN) + trailing)
    blocks = jnp.swapaxes(blocks, 2, 3)
    return blocks.reshape((image_count * per_side * per_side, WIN * WIN) + trailing)


def from_windows(blocks, image_count):
    per_side = SIDE // WIN
    trailing = blocks.shape[2:]
    grid_data = blocks.reshape((image_count, per_side, per_side, WIN, WIN) + trailing)
    grid_data = jnp.swapaxes(grid_data, 2, 3)
    return grid_data.reshape((image_count, SIDE, SIDE) + trailing)


def onehot_table():
    cell_ids = jnp.arange(WIN * WIN)
    cell_row = cell_ids // WIN
    cell_col = cell_ids % WIN
    table_side = 2 * WIN - 1
    rel_index = (cell_row[:, None] - cell_row[None, :] + WIN - 1) * table_side + (
        cell_col[:, None] - cell_col[None, :] + WIN - 1
    )
    rel_index = rel_index.reshape(-1)
    return (rel_index[:, None] == jnp.arange(table_side * table_side)[None, :]).astype(jnp.float32)


def replica_total(stacked):
    return (
        lax.psum(stacked[0].astype(jnp.bfloat16), "rep").astype(jnp.float32),
        lax.psum(stacked[1].astype(jnp.bfloat16), "rep").astype(jnp.float32),
        lax.psum(stacked[2].astype(jnp.bfloat16), "rep").astype(jnp.float32),
        lax.psum(stacked[3].astype(jnp.bfloat16), "rep").astype(jnp.float32),
        lax.psum(stacked[4].astype(jnp.bfloat16), "rep").astype(jnp.float32),
        lax.psum(stacked[5].astype(jnp.bfloat16), "rep").astype(jnp.float32),
        lax.psum(stacked[6].astype(jnp.bfloat16), "rep").astype(jnp.float32),
        lax.psum(stacked[7].astype(jnp.bfloat16), "rep").astype(jnp.float32),
    )


def body(
    images,
    cotangent,
    regions,
    w_qkv,
    w_proj,
    w_fc1,
    w_fc2,
    norm_gains,
    norm_shifts,
    branch_biases,
    fc1_bias,
    rel_table,
):
    layer_count = w_qkv.shape[0]
    image_count = images.shape[0]
    model_width = w_proj.shape[2]
    head_count = rel_table.shape[2]
    head_dim = model_width // head_count
    query_scale = head_dim ** (-0.5)
    column_scale = jnp.concatenate(
        [
            jnp.full((model_width,), query_scale, jnp.float32),
            jnp.ones((2 * model_width,), jnp.float32),
        ]
    )
    onehot = onehot_table()
    region_win = to_windows(regions)
    region_mask = jnp.where(region_win[:, :, None] == region_win[:, None, :], 0.0, -100.0).astype(
        jnp.float32
    )
    window_count = region_win.shape[0]
    tokens = window_count * WIN * WIN

    def score_bias(layer_num):
        table_rows = jnp.dot(onehot, rel_table[layer_num].astype(jnp.float32), precision=highest)
        bias_full = table_rows.T.reshape(head_count, WIN * WIN, WIN * WIN)[None]
        if layer_num % 2 == 1:
            bias_full = bias_full + region_mask[:, None]
        return bias_full

    def heads_of(flat):
        return flat.reshape(window_count, WIN * WIN, head_count, head_dim)

    residual = images.astype(jnp.float32)
    saved_acts = []
    kept_weights = []
    for layer_num in range(layer_count):
        shifted = layer_num % 2 == 1
        attn_w = (
            lax.all_gather(w_qkv[layer_num], "shard", axis=0, tiled=True),
            lax.all_gather(w_proj[layer_num], "shard", axis=0, tiled=True),
            lax.all_gather(norm_gains[layer_num], "shard", axis=1, tiled=True),
            lax.all_gather(norm_shifts[layer_num], "shard", axis=1, tiled=True),
            lax.all_gather(branch_biases[layer_num], "shard", axis=1, tiled=True),
        )
        mlp_w = (
            lax.all_gather(w_fc1[layer_num], "shard", axis=0, tiled=True),
            lax.all_gather(w_fc2[layer_num], "shard", axis=0, tiled=True),
            lax.all_gather(fc1_bias[layer_num], "shard", axis=0, tiled=True),
        )
        kept_weights.append((attn_w, mlp_w))
        wqkv, wproj, gains, shifts, biases = attn_w
        gains = gains.astype(jnp.float32)
        shifts = shifts.astype(jnp.float32)
        biases = biases.astype(jnp.float32)
        normed = layer_norm(residual, gains[0], shifts[0]).astype(jnp.bfloat16)
        if shifted:
            normed = jnp.roll(normed, (-SHIFT, -SHIFT), axis=(1, 2))
        window_rows = to_windows(normed).reshape(tokens, model_width)
        projected = jnp.dot(window_rows, wqkv, preferred_element_type=jnp.float32)
        queries = heads_of(
            ((projected[:, :model_width] + biases[0]) * query_scale).astype(jnp.bfloat16)
        )
        key_rows = heads_of(projected[:, model_width : 2 * model_width].astype(jnp.bfloat16))
        values = heads_of((projected[:, 2 * model_width :] + biases[1]).astype(jnp.bfloat16))
        scores = jnp.einsum(
            "nqhd,nkhd->nhqk", queries, key_rows, preferred_element_type=jnp.float32
        ) + score_bias(layer_num)
        row_max = jnp.max(scores, axis=-1, keepdims=True)
        log_total = row_max + jnp.log(jnp.sum(jnp.exp(scores - row_max), axis=-1, keepdims=True))
        attn_probs = jnp.exp(scores - log_total).astype(jnp.bfloat16)
        mixed_rows = jnp.einsum(
            "nhqk,nkhd->nqhd", attn_probs, values, preferred_element_type=jnp.float32
        )
        mixed_rows = mixed_rows.reshape(tokens, model_width).astype(jnp.bfloat16)
        branch = jnp.dot(mixed_rows, wproj, preferred_element_type=jnp.float32) + biases[2]
        branch = from_windows(branch.reshape(window_count, WIN * WIN, model_width), image_count)
        if shifted:
            branch = jnp.roll(branch, (SHIFT, SHIFT), axis=(1, 2))
        middle = residual + branch
        wfirst, wsecond, bias_first = mlp_w
        normed_mlp = (
            layer_norm(middle, gains[1], shifts[1]).astype(jnp.bfloat16).reshape(-1, model_width)
        )
        pre_act = jnp.dot(
            normed_mlp, wfirst, preferred_element_type=jnp.float32
        ) + bias_first.astype(jnp.float32)
        activated = jax.nn.gelu(pre_act, approximate=False).astype(jnp.bfloat16)
        mlp_out = jnp.dot(activated, wsecond, preferred_element_type=jnp.float32) + biases[3]
        saved_acts.append(
            (
                residual,
                window_rows,
                queries,
                key_rows,
                values,
                log_total,
                mixed_rows,
                middle,
                normed_mlp,
                pre_act,
                activated,
            )
        )
        residual = middle + mlp_out.reshape(middle.shape)
    images_out = residual.astype(jnp.bfloat16)
    upstream = cotangent.astype(jnp.float32)
    layer_grads = [None] * layer_count
    table_list = [None] * layer_count
    for layer_num in reversed(range(layer_count)):
        shifted = layer_num % 2 == 1
        (
            residual_in,
            window_rows,
            queries,
            key_rows,
            values,
            log_total,
            mixed_rows,
            middle,
            normed_mlp,
            pre_act,
            activated,
        ) = saved_acts[layer_num]
        wqkv, wproj, gains, shifts, biases = (
            lax.all_gather(w_qkv[layer_num], "shard", axis=0, tiled=True),
            lax.all_gather(w_proj[layer_num], "shard", axis=0, tiled=True),
            lax.all_gather(norm_gains[layer_num], "shard", axis=1, tiled=True),
            lax.all_gather(norm_shifts[layer_num], "shard", axis=1, tiled=True),
            lax.all_gather(branch_biases[layer_num], "shard", axis=1, tiled=True),
        )
        wfirst, wsecond, bias_first = (
            lax.all_gather(w_fc1[layer_num], "shard", axis=0, tiled=True),
            lax.all_gather(w_fc2[layer_num], "shard", axis=0, tiled=True),
            lax.all_gather(fc1_bias[layer_num], "shard", axis=0, tiled=True),
        )
        gains = gains.astype(jnp.float32)
        shifts = shifts.astype(jnp.float32)
        out_grad = upstream.astype(jnp.bfloat16).reshape(-1, model_width)
        grad_b_second = jnp.sum(out_grad.astype(jnp.float32), axis=0)
        grad_w_second = transposed_times(activated, out_grad)
        act_grad = times_transposed(out_grad, wsecond)
        pre_grad = (act_grad * gelu_slope(pre_act)).astype(jnp.bfloat16)
        grad_b_first = jnp.sum(pre_grad.astype(jnp.float32), axis=0)
        grad_w_first = transposed_times(normed_mlp, pre_grad)
        norm_grad = times_transposed(pre_grad, wfirst).reshape(middle.shape)
        norm_pull = jax.vjp(layer_norm, middle, gains[1], shifts[1])[1]
        middle_part, grad_gain_mlp, grad_shift_mlp = norm_pull(norm_grad)
        middle_grad = upstream + middle_part
        branch_grad = middle_grad
        if shifted:
            branch_grad = jnp.roll(branch_grad, (-SHIFT, -SHIFT), axis=(1, 2))
        branch_rows = to_windows(branch_grad.astype(jnp.bfloat16)).reshape(tokens, model_width)
        grad_b_proj = jnp.sum(branch_rows.astype(jnp.float32), axis=0)
        grad_w_proj = transposed_times(mixed_rows, branch_rows)
        mixed_grad = heads_of(times_transposed(branch_rows, wproj).astype(jnp.bfloat16))
        scores = jnp.einsum(
            "nqhd,nkhd->nhqk", queries, key_rows, preferred_element_type=jnp.float32
        ) + score_bias(layer_num)
        attn_probs = jnp.exp(scores - log_total)
        prob_grad = jnp.einsum(
            "nqhd,nkhd->nhqk", mixed_grad, values, preferred_element_type=jnp.float32
        )
        value_grad = jnp.einsum(
            "nhqk,nqhd->nkhd",
            attn_probs.astype(jnp.bfloat16),
            mixed_grad,
            preferred_element_type=jnp.float32,
        ).astype(jnp.bfloat16)
        score_grad = (
            attn_probs * (prob_grad - jnp.sum(attn_probs * prob_grad, axis=-1, keepdims=True))
        ).astype(jnp.bfloat16)
        table_term = jnp.sum(score_grad.astype(jnp.float32), axis=0).reshape(head_count, -1).T
        table_list[layer_num] = jnp.dot(onehot.T, table_term, precision=highest)
        query_grad = jnp.einsum(
            "nhqk,nkhd->nqhd", score_grad, key_rows, preferred_element_type=jnp.float32
        ).astype(jnp.bfloat16)
        key_grad = jnp.einsum(
            "nhqk,nqhd->nkhd", score_grad, queries, preferred_element_type=jnp.float32
        ).astype(jnp.bfloat16)
        qkv_grad = jnp.concatenate(
            [
                query_grad.reshape(tokens, model_width),
                key_grad.reshape(tokens, model_width),
                value_grad.reshape(tokens, model_width),
            ],
            axis=1,
        )
        grad_w_proj_qkv = transposed_times(window_rows, qkv_grad) * column_scale[None, :]
        grad_b_query = (
            jnp.sum(query_grad.reshape(tokens, model_width).astype(jnp.float32), axis=0)
            * query_scale
        )
        grad_b_value = jnp.sum(value_grad.reshape(tokens, model_width).astype(jnp.float32), axis=0)
        rows_grad = times_transposed(qkv_grad[:, :model_width], wqkv[:, :model_width]) * query_scale
        rows_grad = rows_grad + times_transposed(qkv_grad[:, model_width:], wqkv[:, model_width:])
        normed_grad = from_windows(
            rows_grad.reshape(window_count, WIN * WIN, model_width), image_count
        )
        if shifted:
            normed_grad = jnp.roll(normed_grad, (SHIFT, SHIFT), axis=(1, 2))
        first_pull = jax.vjp(layer_norm, residual_in, gains[0], shifts[0])[1]
        input_part, grad_gain_attn, grad_shift_attn = first_pull(normed_grad)
        upstream = middle_grad + input_part
        gain_grads = jnp.stack([grad_gain_attn, grad_gain_mlp])
        shift_grads = jnp.stack([grad_shift_attn, grad_shift_mlp])
        bias_grads = jnp.stack([grad_b_query, grad_b_value, grad_b_proj, grad_b_second])
        qkv_share, proj_share, gain_share, shift_share, bias_share = (
            lax.psum_scatter(
                grad_w_proj_qkv.astype(jnp.bfloat16), "shard", scatter_dimension=0, tiled=True
            ).astype(jnp.float32),
            lax.psum_scatter(
                grad_w_proj.astype(jnp.bfloat16), "shard", scatter_dimension=0, tiled=True
            ).astype(jnp.float32),
            lax.psum_scatter(
                gain_grads.astype(jnp.bfloat16), "shard", scatter_dimension=1, tiled=True
            ).astype(jnp.float32),
            lax.psum_scatter(
                shift_grads.astype(jnp.bfloat16), "shard", scatter_dimension=1, tiled=True
            ).astype(jnp.float32),
            lax.psum_scatter(
                bias_grads.astype(jnp.bfloat16), "shard", scatter_dimension=1, tiled=True
            ).astype(jnp.float32),
        )
        first_share, second_share, bfirst_share = (
            lax.psum_scatter(
                grad_w_first.astype(jnp.bfloat16), "shard", scatter_dimension=0, tiled=True
            ).astype(jnp.float32),
            lax.psum_scatter(
                grad_w_second.astype(jnp.bfloat16), "shard", scatter_dimension=0, tiled=True
            ).astype(jnp.float32),
            lax.psum_scatter(
                grad_b_first.astype(jnp.bfloat16), "shard", scatter_dimension=0, tiled=True
            ).astype(jnp.float32),
        )
        layer_grads[layer_num] = (
            qkv_share,
            proj_share,
            first_share,
            second_share,
            gain_share,
            shift_share,
            bias_share,
            bfirst_share,
        )
    stacked = [jnp.stack([layer_grads[n][m] for n in range(layer_count)]) for m in range(8)]
    summed = replica_total(stacked)
    table_total = lax.psum(jnp.stack(table_list), ("rep", "shard"))
    return (
        images_out,
        upstream,
        summed[0],
        summed[1],
        summed[2],
        summed[3],
        summed[4],
        summed[5],
        summed[6],
        summed[7],
        table_total,
    )


def solution(mesh):
    return jax.shard_map(
        body,
        mesh=mesh,
        in_specs=(
            P(("rep", "shard"), None, None, None),
            P(("rep", "shard"), None, None, None),
            P(("rep", "shard"), None, None),
            P(None, "shard", None),
            P(None, "shard", None),
            P(None, "shard", None),
            P(None, "shard", None),
            P(None, None, "shard"),
            P(None, None, "shard"),
            P(None, None, "shard"),
            P(None, "shard"),
            P(),
        ),
        out_specs=(
            P(("rep", "shard"), None, None, None),
            P(("rep", "shard"), None, None, None),
            P(None, "shard", None),
            P(None, "shard", None),
            P(None, "shard", None),
            P(None, "shard", None),
            P(None, None, "shard"),
            P(None, None, "shard"),
            P(None, None, "shard"),
            P(None, "shard"),
            P(),
        ),
        check_vma=False,
    )
```

profile of v0, /device:TPU:0, one launch (start us, length us, event | category | flops | bytes accessed | tf_op | source)
XLA Modules:
  0.0 1341.8 jit_solution(16533433941194631323)
XLA Ops:
  17.5 24.0 %all-gather = bf16[1,2,512]{1,0,2:T(2,128)(2,1)S(1)} all-gather(bf16[1,2,32]{1,0,2:T(2,128)(2,1)S(1)} %copy.412), channel_id=2, replica_groups=mesh['rep'=2,'shard'=16] {'shard'}, dimensions={2}, use_global_device_ids=true | all-gather | bytes 2176 | tf_op jit(solution)/shard_map/all_gather | solution.py:134
  41.7 2.7 slice_reduce_fusion.10
  44.6 18.3 %all-gather.1 = bf16[1,2,512]{1,0,2:T(2,128)(2,1)S(1)} all-gather(bf16[1,2,32]{1,0,2:T(2,128)(2,1)S(1)} %copy.413), channel_id=3, replica_groups=mesh['rep'=2,'shard'=16] {'shard'}, dimensions={2}, use_global_device_ids=true | all-gather | bytes 2176 | tf_op jit(solution)/shard_map/all_gather | solution.py:135
  63.1 2.7 slice_reduce_fusion.9
  67.9 20.7 %all-gather.3 = bf16[1,4,512]{1,0,2:T(2,128)(2,1)S(1)} all-gather(bf16[1,4,32]{1,0,2:T(2,128)(2,1)S(1)} %copy.414), channel_id=5, replica_groups=mesh['rep'=2,'shard'=16] {'shard'}, dimensions={2}, use_global_device_ids=true | all-gather | bytes 4352 | tf_op jit(solution)/shard_map/all_gather | solution.py:136
  88.9 6.7 slice_reduce_fusion.8
  96.1 19.4 %all-gather.4 = bf16[1,512,512]{2,1,0:T(8,128)(2,1)S(1)} all-gather(bf16[1,32,512]{2,1,0:T(8,128)(2,1)S(1)} %get-tuple-element.155), channel_id=6, replica_groups=mesh['rep'=2,'shard'=16] {'shard'}, dimensions={1}, use_global_device_ids=true | all-gather | bytes 557056 | tf_op jit(solution)/shard_map/all_gather | solution.py:133
  115.5 18.6 %all-gather.6 = bf16[1,2048]{1,0:T(2,128)(2,1)S(1)} all-gather(bf16[1,128]{1,0:T(2,128)(2,1)S(1)} %get-tuple-element.163), channel_id=8, replica_groups=mesh['rep'=2,'shard'=16] {'shard'}, dimensions={1}, use_global_device_ids=true | all-gather | bytes 4352 | tf_op jit(solution)/shard_map/all_gather | solution.py:141
  134.3 18.2 %all-gather.8 = bf16[1,2,512]{1,0,2:T(2,128)(2,1)S(1)} all-gather(bf16[1,2,32]{1,0,2:T(2,128)(2,1)S(1)} %copy.415), channel_id=10, replica_groups=mesh['rep'=2,'shard'=16] {'shard'}, dimensions={2}, use_global_device_ids=true | all-gather | bytes 2176 | tf_op jit(solution)/shard_map/all_gather | solution.py:134
  152.7 3.3 slice_reduce_fusion.2
  156.2 19.6 %all-gather.9 = bf16[1,2,512]{1,0,2:T(2,128)(2,1)S(1)} all-gather(bf16[1,2,32]{1,0,2:T(2,128)(2,1)S(1)} %copy.416), channel_id=11, replica_groups=mesh['rep'=2,'shard'=16] {'shard'}, dimensions={2}, use_global_device_ids=true | all-gather | bytes 2176 | tf_op jit(solution)/shard_map/all_gather | solution.py:135
  176.0 3.3 slice_reduce_fusion.1
  179.4 31.4 %all-gather.11 = bf16[1,4,512]{1,0,2:T(2,128)(2,1)S(1)} all-gather(bf16[1,4,32]{1,0,2:T(2,128)(2,1)S(1)} %copy.417), channel_id=13, replica_groups=mesh['rep'=2,'shard'=16] {'shard'}, dimensions={2}, use_global_device_ids=true | all-gather | bytes 4352 | tf_op jit(solution)/shard_map/all_gather | solution.py:136
  211.1 7.3 slice_reduce_fusion
  220.6 21.8 %all-gather.12 = bf16[1,512,512]{2,1,0:T(8,128)(2,1)} all-gather(bf16[1,32,512]{2,1,0:T(8,128)(2,1)S(1)} %get-tuple-element.154), channel_id=14, replica_groups=mesh['rep'=2,'shard'=16] {'shard'}, dimensions={1}, use_global_device_ids=true | all-gather | bytes 557056 | tf_op jit(solution)/shard_map/all_gather | solution.py:133
  242.4 17.3 %all-gather.14 = bf16[1,2048]{1,0:T(2,128)(2,1)S(1)} all-gather(bf16[1,128]{1,0:T(2,128)(2,1)S(1)} %get-tuple-element.162), channel_id=16, replica_groups=mesh['rep'=2,'shard'=16] {'shard'}, dimensions={1}, use_global_device_ids=true | all-gather | bytes 4352 | tf_op jit(solution)/shard_map/all_gather | solution.py:141
  271.0 2.6 copy.312
  283.9 7.4 fusion.20
  291.3 3.2 fusion.57
  305.0 2.6 copy.324
  309.0 2.6 copy.325
  311.6 2.3 reshape.792
  313.9 2.6 copy.328
  334.2 7.0 fusion.23
  341.3 3.9 fusion.150
  347.4 2.2 reshape.795
  349.6 4.6 multiply_reduce_fusion.2
  354.8 3.2 fusion.60
  358.0 2.3 reshape.774
  360.3 5.4 fusion.130
  377.5 2.3 reshape.796
  379.9 2.6 copy.337
  382.5 2.7 multiply_reduce_fusion.1
  394.1 2.2 copy.347
  398.5 2.2 copy.341
  404.3 2.7 convolution_add_fusion.3
  414.6 4.8 multiply_reduce_fusion.3
  419.4 4.3 fusion.129
  423.8 2.7 convert_reduce_fusion.6
  426.5 3.9 fusion.151
  432.3 3.7 multiply_reduce_fusion.4
  436.1 3.4 fusion.128
  439.5 2.7 convert_reduce_fusion.4
  443.4 2.3 reshape.798
  447.5 3.4 multiply_reduce_fusion
  451.2 3.0 convert_reduce_fusion.1
  490.2 3.1 multiply_reduce_fusion.5
  493.4 3.4 fusion.127
  497.7 31.7 %all-reduce.2 = (bf16[2048]{0:T(1024)(128)(2,1)S(1)}, bf16[2048]{0:T(1024)(128)(2,1)S(1)}) all-reduce(bf16[2048]{0:T(1024)(128)(2,1)S(1)} %copy-done.107, bf16[2048]{0:T(1024)(128)(2,1)S(1)} %copy-done.108), channel_id=33, replica_groups=mesh['rep'=2,'shard'=16] {'shard'}, use_global_device_ids=true, to_apply=%region_63.64.clone | all-reduce | flops 4096 | bytes 16384
  534.4 37.7 %psum.71 = f32[2,169,16]{1,2,0:T(8,128)} all-reduce(f32[2,169,16]{1,2,0:T(8,128)S(1)} %pad_maximum_fusion.10), channel_id=1, replica_groups=mesh['rep'=2,'shard'=16] {'rep','shard'}, use_global_device_ids=true, to_apply=%region_67.68 | all-reduce | flops 5408 | bytes 43264 | tf_op jit(solution)/shard_map/psum | solution.py:340
  573.6 53.1 %reduce-scatter.27.cloned.1.call-done = bf16[32,1536]{1,0:T(8,128)(2,1)} async-done(((bf16[512,1536]{1,0:T(8,128)(2,1)}), bf16[32,1536]{1,0:T(8,128)(2,1)}) %reduce-scatter.27.cloned.1.call-update) | async-done | bytes 98320 | tf_op jit(solution)/shard_map/reduce_scatter | solution.py:301
  626.7 62.5 %reduce-scatter.29.cloned.1.call-done = bf16[32,1536]{1,0:T(8,128)(2,1)} async-done(((bf16[512,1536]{1,0:T(8,128)(2,1)}), bf16[32,1536]{1,0:T(8,128)(2,1)}) %reduce-scatter.29.cloned.1.call-update) | async-done | bytes 98320 | tf_op jit(solution)/shard_map/reduce_scatter | solution.py:301
  690.8 62.7 %reduce-scatter.37.cloned.1.call-done = bf16[32,2048]{1,0:T(8,128)(2,1)} async-done(((bf16[512,2048]{1,0:T(8,128)(2,1)}), bf16[32,2048]{1,0:T(8,128)(2,1)}) %reduce-scatter.37.cloned.1.call-update) | async-done | bytes 131088 | tf_op jit(solution)/shard_map/reduce_scatter | solution.py:318
  753.6 64.6 %reduce-scatter.35.cloned.1.call-done = bf16[32,2048]{1,0:T(8,128)(2,1)} async-done(((bf16[512,2048]{1,0:T(8,128)(2,1)}), bf16[32,2048]{1,0:T(8,128)(2,1)}) %reduce-scatter.35.cloned.1.call-update) | async-done | bytes 131088 | tf_op jit(solution)/shard_map/reduce_scatter | solution.py:318
  819.9 62.6 %reduce-scatter.39.cloned.1.call-done = bf16[128,512]{1,0:T(8,128)(2,1)} async-done(((bf16[2048,512]{1,0:T(8,128)(2,1)}), bf16[128,512]{1,0:T(8,128)(2,1)}) %reduce-scatter.39.cloned.1.call-update) | async-done | bytes 131088 | tf_op jit(solution)/shard_map/reduce_scatter | solution.py:321
  882.4 64.7 %reduce-scatter.41.cloned.1.call-done = bf16[128,512]{1,0:T(8,128)(2,1)} async-done(((bf16[2048,512]{1,0:T(8,128)(2,1)}), bf16[128,512]{1,0:T(8,128)(2,1)}) %reduce-scatter.41.cloned.1.call-update) | async-done | bytes 131088 | tf_op jit(solution)/shard_map/reduce_scatter | solution.py:321
  950.1 54.4 %reduce-scatter.47.cloned.1.call-done = bf16[32,2]{1,0:T(8,128)(2,1)} async-done(((bf16[512,2]{1,0:T(8,128)(2,1)}), bf16[32,2]{1,0:T(8,128)(2,1)}) %reduce-scatter.47.cloned.1.call-update) | async-done | bytes 144
  1005.3 56.7 %reduce-scatter.49.cloned.1.call-done = bf16[32,2]{1,0:T(8,128)(2,1)} async-done(((bf16[512,2]{1,0:T(8,128)(2,1)}), bf16[32,2]{1,0:T(8,128)(2,1)}) %reduce-scatter.49.cloned.1.call-update) | async-done | bytes 144
  1062.8 56.7 %reduce-scatter.43.cloned.1.call-done = bf16[32,2]{1,0:T(8,128)(2,1)} async-done(((bf16[512,2]{1,0:T(8,128)(2,1)}), bf16[32,2]{1,0:T(8,128)(2,1)}) %reduce-scatter.43.cloned.1.call-update) | async-done | bytes 144
  1120.2 57.2 %reduce-scatter.45.cloned.1.call-done = bf16[32,2]{1,0:T(8,128)(2,1)} async-done(((bf16[512,2]{1,0:T(8,128)(2,1)}), bf16[32,2]{1,0:T(8,128)(2,1)}) %reduce-scatter.45.cloned.1.call-update) | async-done | bytes 144
  1178.3 56.8 %reduce-scatter.51.cloned.1.call-done = bf16[32,4]{1,0:T(8,128)(2,1)} async-done(((bf16[512,4]{1,0:T(8,128)(2,1)}), bf16[32,4]{1,0:T(8,128)(2,1)}) %reduce-scatter.51.cloned.1.call-update) | async-done | bytes 272
  1235.8 56.7 %reduce-scatter.53.cloned.1.call-done = bf16[32,4]{1,0:T(8,128)(2,1)} async-done(((bf16[512,4]{1,0:T(8,128)(2,1)}), bf16[32,4]{1,0:T(8,128)(2,1)}) %reduce-scatter.53.cloned.1.call-update) | async-done | bytes 272
  1293.3 5.0 all-reduce.3
  1300.6 28.8 %all-reduce.7.cloned.1.call-done = (bf16[2,32,1536]{2,1,0:T(8,128)(2,1)}, bf16[2,32,512]{2,1,0:T(8,128)(2,1)}, bf16[2,32,2048]{2,1,0:T(8,128)(2,1)}, bf16[2,128,512]{2,1,0:T(8,128)(2,1)}) async-done(((bf16[2,32,1536]{2,1,0:T(8,128)(2,1)}, bf16[2,32,512]{2,1,0:T(8,128)(2,1)}, bf16[2,32,2048]{2,1,0:T(8,128)(2,1)}, bf16[2,128,512]{2,1,0:T(8,128)(2,1)}), (bf16[2,32,1536]{2,1,0:T(8,128)(2,1)}, ...) | async-done | bytes 786448 | tf_op jit(solution)/shard_map/psum | solution.py:71
  (516 shorter events, 169.8 us)
Async XLA Ops:
  7.2 7.3 copy-start.113
  7.2 253.9 %all-gather.23.cloned.1.call-start = ((), (), s32[]{:S(2)}) async-start(), calls=%async_computation.22 | async-start | bytes 1671168 | tf_op jit(solution)/shard_map/all_gather | solution.py:132
  8.9 6.8 copy-start.2
  8.9 275.0 %all-gather.25.cloned.1.call-start = ((), (), s32[]{:S(2)}) async-start(), calls=%async_computation.23 | async-start | bytes 2228224 | tf_op jit(solution)/shard_map/all_gather | solution.py:139
  10.7 6.7 copy-start.111
  10.7 280.6 %all-gather.27.cloned.1.call-start = ((), (), s32[]{:S(2)}) async-start(), calls=%async_computation.24 | async-start | bytes 2228224 | tf_op jit(solution)/shard_map/all_gather | solution.py:140
  12.4 288.5 %all-gather.29.cloned.1.call-start = ((), (), s32[]{:S(2)}) async-start(), calls=%async_computation.25 | async-start | bytes 1671168 | tf_op jit(solution)/shard_map/all_gather | solution.py:132
  13.0 321.2 %all-gather.31.cloned.1.call-start = ((), (), s32[]{:S(2)}) async-start(), calls=%async_computation.26 | async-start | bytes 2228224 | tf_op jit(solution)/shard_map/all_gather | solution.py:139
  13.6 327.7 %all-gather.33.cloned.1.call-start = ((), (), s32[]{:S(2)}) async-start(), calls=%async_computation.27 | async-start | bytes 2228224 | tf_op jit(solution)/shard_map/all_gather | solution.py:140
  14.2 558.0 %reduce-scatter.33.cloned.1.call-start = ((), (), s32[]{:S(2)}) async-start(), calls=%async_computation.17 | async-start | bytes 557056 | tf_op jit(solution)/shard_map/reduce_scatter | solution.py:304
  14.3 30.1 %copy-start.112 = (bf16[2,2,32]{2,1,0:T(2,128)(2,1)S(1)}, bf16[2,2,32]{2,1,0:T(2,128)(2,1)}, u32[]{:S(2)}) copy-start(bf16[2,2,32]{2,1,0:T(2,128)(2,1)} %param.20) | copy-start | bytes 772
  16.3 49.5 %copy-start.61 = (f32[14,14]{1,0:T(8,128)}, f32[14,14]{1,0:T(8,128)S(1)}, u32[]{:S(2)}) copy-start(f32[14,14]{1,0:T(8,128)S(1)} %broadcast_multiply_fusion.3) | copy-start | bytes 2356
  17.3 50.3 %copy-start.71 = (f32[14,14]{1,0:T(8,128)}, f32[14,14]{1,0:T(8,128)S(1)}, u32[]{:S(2)}) copy-start(f32[14,14]{1,0:T(8,128)S(1)} %multiply_reduce_fusion.13) | copy-start | bytes 2356
  17.3 50.3 %copy-start.69 = (f32[14,14]{1,0:T(8,128)}, f32[14,14]{1,0:T(8,128)S(1)}, u32[]{:S(2)}) copy-start(f32[14,14]{1,0:T(8,128)S(1)} %fusion.110) | copy-start | bytes 2356
  44.5 23.3 %copy-start.79 = (f32[512]{0:T(512)}, f32[512]{0:T(512)S(1)}, u32[]{:S(2)}) copy-start(f32[512]{0:T(512)S(1)} %get-tuple-element.102) | copy-start | bytes 6148
  44.5 238.0 %copy-start.81 = (f32[512]{0:T(512)}, f32[512]{0:T(512)S(1)}, u32[]{:S(2)}) copy-start(f32[512]{0:T(512)S(1)} %get-tuple-element.101) | copy-start | bytes 6148
  44.5 23.3 %copy-start.109 = (bf16[2,4,32]{2,1,0:T(4,128)(2,1)S(1)}, bf16[2,4,32]{2,1,0:T(4,128)(2,1)}, u32[]{:S(2)}) copy-start(bf16[2,4,32]{2,1,0:T(4,128)(2,1)} %param.21) | copy-start | bytes 1540
  67.8 193.3 %copy-start.39 = (bf16[196,512]{1,0:T(8,128)(2,1)}, bf16[196,512]{1,0:T(8,128)(2,1)S(1)}, u32[]{:S(2)}) copy-start(bf16[196,512]{1,0:T(8,128)(2,1)S(1)} %reshape_reshape.24) | copy-start | bytes 602116
  67.9 28.2 %copy-start.78 = (bf16[2,32,512]{2,1,0:T(8,128)(2,1)S(1)}, bf16[2,32,512]{2,1,0:T(8,128)(2,1)}, u32[]{:S(2)}) copy-start(bf16[2,32,512]{2,1,0:T(8,128)(2,1)} %param.16) | copy-start | bytes 196612
  88.9 26.7 %copy-start.110 = (bf16[2,128]{1,0:T(2,128)(2,1)S(1)}, bf16[2,128]{1,0:T(2,128)(2,1)}, u32[]{:S(2)}) copy-start(bf16[2,128]{1,0:T(2,128)(2,1)} %param.22) | copy-start | bytes 1540
  115.5 162.2 %copy-start.4 = (bf16[1,512,512]{2,1,0:T(8,128)(2,1)}, bf16[1,512,512]{2,1,0:T(8,128)(2,1)S(1)}, u32[]{:S(2)}) copy-start(bf16[1,512,512]{2,1,0:T(8,128)(2,1)S(1)} %all-gather.4) | copy-start | bytes 1572868
  156.0 142.1 %copy-start.83 = (f32[512]{0:T(512)}, f32[512]{0:T(512)S(1)}, u32[]{:S(2)}) copy-start(f32[512]{0:T(512)S(1)} %get-tuple-element.94) | copy-start | bytes 6148
  179.4 40.2 %copy-start.97 = (s32[1,14,14]{2,0,1:T(1,128)S(1)}, s32[1,14,14]{2,0,1:T(1,128)}, u32[]{:S(2)}) copy-start(s32[1,14,14]{2,0,1:T(1,128)} %param.14) | copy-start | bytes 2356
  211.1 49.2 %copy-start.25 = (bf16[1,14,14,512]{3,2,1,0:T(8,128)(2,1)S(1)}, bf16[1,14,14,512]{3,2,1,0:T(8,128)(2,1)}, u32[]{:S(2)}) copy-start(bf16[1,14,14,512]{3,2,1,0:T(8,128)(2,1)} %param.13) | copy-start | bytes 602116
  269.6 5.5 copy-start.37
  283.9 7.4 copy-start.42
  309.0 7.5 copy-start.31
  323.0 5.7 copy-start.21
  354.8 5.4 copy-start.86
  360.3 5.4 copy-start.26
  408.8 4.8 copy-start.28
  410.5 8.9 copy-start.76
  432.3 7.2 copy-start.35
  442.4 8.6 copy-start.29
  442.4 5.1 copy-start.6
  450.9 121.3 %reduce-scatter.31.cloned.1.call-start = ((), (), s32[]{:S(2)}) async-start(), calls=%async_computation.16 | async-start | bytes 557056 | tf_op jit(solution)/shard_map/reduce_scatter | solution.py:304
  454.8 5.4 copy-start.38
  460.2 166.5 %reduce-scatter.27.cloned.1.call-start = ((), (), s32[]{:S(2)}) async-start(), calls=%async_computation.14 | async-start | bytes 1671168 | tf_op jit(solution)/shard_map/reduce_scatter | solution.py:301
  466.2 223.0 %reduce-scatter.29.cloned.1.call-start = ((), (), s32[]{:S(2)}) async-start(), calls=%async_computation.15 | async-start | bytes 1671168 | tf_op jit(solution)/shard_map/reduce_scatter | solution.py:301
  468.1 285.4 %reduce-scatter.37.cloned.1.call-start = ((), (), s32[]{:S(2)}) async-start(), calls=%async_computation.19 | async-start | bytes 2228224 | tf_op jit(solution)/shard_map/reduce_scatter | solution.py:318
  471.4 346.8 %reduce-scatter.35.cloned.1.call-start = ((), (), s32[]{:S(2)}) async-start(), calls=%async_computation.18 | async-start | bytes 2228224 | tf_op jit(solution)/shard_map/reduce_scatter | solution.py:318
  474.6 407.8 %reduce-scatter.39.cloned.1.call-start = ((), (), s32[]{:S(2)}) async-start(), calls=%async_computation.20 | async-start | bytes 2228224 | tf_op jit(solution)/shard_map/reduce_scatter | solution.py:321
  478.0 469.1 %reduce-scatter.41.cloned.1.call-start = ((), (), s32[]{:S(2)}) async-start(), calls=%async_computation.21 | async-start | bytes 2228224 | tf_op jit(solution)/shard_map/reduce_scatter | solution.py:321
  481.4 523.2 %reduce-scatter.47.cloned.1.call-start = ((), (), s32[]{:S(2)}) async-start(), calls=%async_computation.30 | async-start | bytes 139264
  487.7 5.6 copy-start.72
  488.2 9.5 copy-start.105
  488.2 9.5 copy-start.107
  488.2 9.5 copy-start.108
  489.1 41.2 %copy-start.103 = (bf16[512]{0:T(512)(128)(2,1)S(1)}, bf16[512]{0:T(512)(128)(2,1)}, u32[]{:S(2)}) copy-start(bf16[512]{0:T(512)(128)(2,1)} %get-tuple-element.79) | copy-start | bytes 3076
  489.1 41.2 %copy-start.98 = (bf16[512]{0:T(512)(128)(2,1)S(1)}, bf16[512]{0:T(512)(128)(2,1)}, u32[]{:S(2)}) copy-start(bf16[512]{0:T(512)(128)(2,1)} %get-tuple-element.81) | copy-start | bytes 3076
  489.1 41.6 %copy-start.104 = (bf16[512]{0:T(512)(128)(2,1)S(1)}, bf16[512]{0:T(512)(128)(2,1)}, u32[]{:S(2)}) copy-start(bf16[512]{0:T(512)(128)(2,1)} %get-tuple-element.85) | copy-start | bytes 3076
  489.1 41.6 %copy-start.102 = (bf16[512]{0:T(512)(128)(2,1)S(1)}, bf16[512]{0:T(512)(128)(2,1)}, u32[]{:S(2)}) copy-start(bf16[512]{0:T(512)(128)(2,1)} %get-tuple-element.87) | copy-start | bytes 3076
  489.2 41.6 %copy-start.99 = (bf16[512]{0:T(512)(128)(2,1)S(1)}, bf16[512]{0:T(512)(128)(2,1)}, u32[]{:S(2)}) copy-start(bf16[512]{0:T(512)(128)(2,1)} %get-tuple-element.119) | copy-start | bytes 3076
  489.2 41.6 %copy-start.100 = (bf16[512]{0:T(512)(128)(2,1)S(1)}, bf16[512]{0:T(512)(128)(2,1)}, u32[]{:S(2)}) copy-start(bf16[512]{0:T(512)(128)(2,1)} %get-tuple-element.145) | copy-start | bytes 3076
  489.2 41.6 %copy-start.87 = (bf16[16,32]{1,0:T(8,128)(2,1)S(1)}, bf16[16,32]{1,0:T(8,128)(2,1)}, u32[]{:S(2)}) copy-start(bf16[16,32]{1,0:T(8,128)(2,1)} %get-tuple-element.182) | copy-start | bytes 3076
  489.2 42.7 %copy-start.96 = (bf16[1,512]{1,0:T(2,128)(2,1)S(1)}, bf16[1,512]{1,0:T(2,128)(2,1)}, u32[]{:S(2)}) copy-start(bf16[1,512]{1,0:T(2,128)(2,1)} %stack.220) | copy-start | bytes 3076
  490.1 43.4 %copy-start.33 = (bf16[1,14,14,512]{3,0,2,1:T(2,128)(2,1)S(1)}, bf16[1,14,14,512]{3,0,2,1:T(2,128)(2,1)}, u32[]{:S(2)}) copy-start(bf16[1,14,14,512]{3,0,2,1:T(2,128)(2,1)} %get-tuple-element.147) | copy-start | bytes 602116
  496.8 565.2 %reduce-scatter.49.cloned.1.call-start = ((), (), s32[]{:S(2)}) async-start(), calls=%async_computation.31 | async-start | bytes 139264
  529.4 590.0 %reduce-scatter.43.cloned.1.call-start = ((), (), s32[]{:S(2)}) async-start(), calls=%async_computation.28 | async-start | bytes 139264
  530.4 647.1 %reduce-scatter.45.cloned.1.call-start = ((), (), s32[]{:S(2)}) async-start(), calls=%async_computation.29 | async-start | bytes 139264
  531.8 703.2 %reduce-scatter.51.cloned.1.call-start = ((), (), s32[]{:S(2)}) async-start(), calls=%async_computation.32 | async-start | bytes 139264
  533.6 415.3 %copy-start.34 = (f32[1,14,14,512]{3,0,2,1:T(1,128)S(1)}, f32[1,14,14,512]{3,0,2,1:T(1,128)}, u32[]{:S(2)}) copy-start(f32[1,14,14,512]{3,0,2,1:T(1,128)} %get-tuple-element.127) | copy-start | bytes 1204228
  534.3 758.2 %reduce-scatter.53.cloned.1.call-start = ((), (), s32[]{:S(2)}) async-start(), calls=%async_computation.33 | async-start | bytes 139264
  572.1 757.3 %all-reduce.7.cloned.1.call-start = ((), (), s32[]{:S(2)}) async-start(), calls=%async_computation.34 | async-start | bytes 1572864 | tf_op jit(solution)/shard_map/psum | solution.py:71
  (73 other events, 160.0 us)
Sparse Core Ops, SparseCore 0:
  10.9 42.7 all-gather.22
  56.4 40.3 all-gather.24
  99.5 40.4 all-gather.26
  142.1 38.9 all-gather.28
  183.7 40.5 all-gather.30
  226.9 40.4 all-gather.32
  451.1 53.9 reduce-scatter.32
  509.6 54.7 reduce-scatter.30
  568.1 58.5 reduce-scatter.26
  630.6 58.4 reduce-scatter.28
  692.9 60.5 reduce-scatter.36
  757.6 60.5 reduce-scatter.34
  821.9 60.4 reduce-scatter.38
  886.5 60.5 reduce-scatter.40
  950.4 54.0 reduce-scatter.46
  1007.8 54.1 reduce-scatter.48
  1065.3 54.0 reduce-scatter.42
  1123.3 54.0 reduce-scatter.44
  1180.9 54.0 reduce-scatter.50
  1238.3 54.0 reduce-scatter.52
  1295.5 33.8 all-reduce.6
where the time goes:
time: 1350 us; the launch traced here: 1340 us
  waiting for transfers between devices  739 us (55%)
  blocking collectives  284 us (21%)
  local copies, waits for them, and re-layouts  132 us (10%)
  other arithmetic  84.2 us (6%)
  matrix products  84.1 us (6%)
  between operations  17.4 us (1%)
    unnamed x27, waiting for transfers between devices  340 us
    reduce_scatter x2, waiting for transfers between devices, body(): lax.psum_scatter(grad_w_first.astype(jnp.bfloat16), 'shard', scatter_dime...  127 us
    reduce_scatter x2, waiting for transfers between devices, body(): lax.psum_scatter(grad_w_second.astype(jnp.bfloat16), 'shard', scatter_dim...  127 us
    reduce_scatter x2, waiting for transfers between devices, body(): lax.psum_scatter(grad_w_proj_qkv.astype(jnp.bfloat16), 'shard', scatter_d...  116 us
    all_gather x2, blocking collectives, body(): lax.all_gather(branch_biases[layer_num], 'shard', axis=1, tiled=True)  52.1 us
    all_gather x2, blocking collectives, body(): lax.all_gather(norm_gains[layer_num], 'shard', axis=1, tiled=True)  42.1 us
    all_gather x2, blocking collectives, body(): lax.all_gather(w_proj[layer_num], 'shard', axis=0, tiled=True)  41.2 us
    all_gather x2, blocking collectives, body(): lax.all_gather(norm_shifts[layer_num], 'shard', axis=1, tiled=True)  37.8 us
  transfers between devices with their start and end apart: 21, of which 13 were waited for; matrix products, arithmetic and copies ran while one was open for 13% of the time, Pallas kernels for 0%

commit v1 on v0

--- a/solution.py
+++ b/solution.py
@@ -337,7 +337,9 @@
         )
     stacked = [jnp.stack([layer_grads[n][m] for n in range(layer_count)]) for m in range(8)]
     summed = replica_total(stacked)
-    table_total = lax.psum(jnp.stack(table_list), ("rep", "shard"))
+    table_total = jnp.stack(table_list)
+    for mesh_axis in ("shard", "rep"):
+        table_total = lax.psum(table_total, mesh_axis)
     return (
         images_out,
         upstream,

time: 1350 us -> 1350 us (level)
  blocking collectives: 284 us -> 313 us
  waiting for transfers between devices: 739 us -> 710 us
    reduce_scatter x2, waiting for transfers between devices: 116 us -> 86.4 us  [body(): lax.psum_scatter(grad_w_proj_qkv.astype(jnp.bfloat16), 'shard', scatter_d...]
    psum x1 -> x2, blocking collectives: 37.7 us -> 66.7 us  [body(): table_total = lax.psum(table_total, mesh_axis)]
where the time goes in v1:
time: 1350 us; the launch traced here: 1340 us
  waiting for transfers between devices  710 us (53%)
  blocking collectives  313 us (23%)
  local copies, waits for them, and re-layouts  131 us (10%)
  matrix products  85.1 us (6%)
  other arithmetic  84.2 us (6%)
  between operations  17.4 us (1%)
    unnamed x27, waiting for transfers between devices  340 us
    reduce_scatter x2, waiting for transfers between devices, body(): lax.psum_scatter(grad_w_second.astype(jnp.bfloat16), 'shard', scatter_dim...  127 us
    reduce_scatter x2, waiting for transfers between devices, body(): lax.psum_scatter(grad_w_first.astype(jnp.bfloat16), 'shard', scatter_dime...  127 us
    reduce_scatter x2, waiting for transfers between devices, body(): lax.psum_scatter(grad_w_proj_qkv.astype(jnp.bfloat16), 'shard', scatter_d...  86.4 us
    psum x2, blocking collectives, body(): table_total = lax.psum(table_total, mesh_axis)  66.7 us
    all_gather x2, blocking collectives, body(): lax.all_gather(branch_biases[layer_num], 'shard', axis=1, tiled=True)  51.7 us
    all_gather x2, blocking collectives, body(): lax.all_gather(norm_gains[layer_num], 'shard', axis=1, tiled=True)  42.7 us
    all_gather x2, blocking collectives, body(): lax.all_gather(w_proj[layer_num], 'shard', axis=0, tiled=True)  41.1 us
  transfers between devices with their start and end apart: 21, of which 13 were waited for; matrix products, arithmetic and copies ran while one was open for 13% of the time, Pallas kernels for 0%

profile of v1, /device:TPU:0, one launch (start us, length us, event | category | flops | bytes accessed | tf_op | source)
XLA Modules:
  0.0 1342.0 jit_solution(1424240670160909906)
XLA Ops:
  17.5 24.1 %all-gather = bf16[1,2,512]{1,0,2:T(2,128)(2,1)S(1)} all-gather(bf16[1,2,32]{1,0,2:T(2,128)(2,1)S(1)} %copy.412), channel_id=2, replica_groups=mesh['rep'=2,'shard'=16] {'shard'}, dimensions={2}, use_global_device_ids=true | all-gather | bytes 2176 | tf_op jit(solution)/shard_map/all_gather | solution.py:134
  41.9 2.7 slice_reduce_fusion.10
  44.8 18.6 %all-gather.1 = bf16[1,2,512]{1,0,2:T(2,128)(2,1)S(1)} all-gather(bf16[1,2,32]{1,0,2:T(2,128)(2,1)S(1)} %copy.413), channel_id=3, replica_groups=mesh['rep'=2,'shard'=16] {'shard'}, dimensions={2}, use_global_device_ids=true | all-gather | bytes 2176 | tf_op jit(solution)/shard_map/all_gather | solution.py:135
  63.6 2.7 slice_reduce_fusion.9
  68.4 20.2 %all-gather.3 = bf16[1,4,512]{1,0,2:T(2,128)(2,1)S(1)} all-gather(bf16[1,4,32]{1,0,2:T(2,128)(2,1)S(1)} %copy.414), channel_id=5, replica_groups=mesh['rep'=2,'shard'=16] {'shard'}, dimensions={2}, use_global_device_ids=true | all-gather | bytes 4352 | tf_op jit(solution)/shard_map/all_gather | solution.py:136
  88.9 6.7 slice_reduce_fusion.8
  96.1 19.5 %all-gather.4 = bf16[1,512,512]{2,1,0:T(8,128)(2,1)S(1)} all-gather(bf16[1,32,512]{2,1,0:T(8,128)(2,1)S(1)} %get-tuple-element.155), channel_id=6, replica_groups=mesh['rep'=2,'shard'=16] {'shard'}, dimensions={1}, use_global_device_ids=true | all-gather | bytes 557056 | tf_op jit(solution)/shard_map/all_gather | solution.py:133
  115.6 18.2 %all-gather.6 = bf16[1,2048]{1,0:T(2,128)(2,1)S(1)} all-gather(bf16[1,128]{1,0:T(2,128)(2,1)S(1)} %get-tuple-element.163), channel_id=8, replica_groups=mesh['rep'=2,'shard'=16] {'shard'}, dimensions={1}, use_global_device_ids=true | all-gather | bytes 4352 | tf_op jit(solution)/shard_map/all_gather | solution.py:141
  133.9 18.6 %all-gather.8 = bf16[1,2,512]{1,0,2:T(2,128)(2,1)S(1)} all-gather(bf16[1,2,32]{1,0,2:T(2,128)(2,1)S(1)} %copy.415), channel_id=10, replica_groups=mesh['rep'=2,'shard'=16] {'shard'}, dimensions={2}, use_global_device_ids=true | all-gather | bytes 2176 | tf_op jit(solution)/shard_map/all_gather | solution.py:134
  152.8 3.3 slice_reduce_fusion.2
  156.2 19.2 %all-gather.9 = bf16[1,2,512]{1,0,2:T(2,128)(2,1)S(1)} all-gather(bf16[1,2,32]{1,0,2:T(2,128)(2,1)S(1)} %copy.416), channel_id=11, replica_groups=mesh['rep'=2,'shard'=16] {'shard'}, dimensions={2}, use_global_device_ids=true | all-gather | bytes 2176 | tf_op jit(solution)/shard_map/all_gather | solution.py:135
  175.7 3.3 slice_reduce_fusion.1
  179.2 31.5 %all-gather.11 = bf16[1,4,512]{1,0,2:T(2,128)(2,1)S(1)} all-gather(bf16[1,4,32]{1,0,2:T(2,128)(2,1)S(1)} %copy.417), channel_id=13, replica_groups=mesh['rep'=2,'shard'=16] {'shard'}, dimensions={2}, use_global_device_ids=true | all-gather | bytes 4352 | tf_op jit(solution)/shard_map/all_gather | solution.py:136
  211.0 7.3 slice_reduce_fusion
  220.4 21.6 %all-gather.12 = bf16[1,512,512]{2,1,0:T(8,128)(2,1)} all-gather(bf16[1,32,512]{2,1,0:T(8,128)(2,1)S(1)} %get-tuple-element.154), channel_id=14, replica_groups=mesh['rep'=2,'shard'=16] {'shard'}, dimensions={1}, use_global_device_ids=true | all-gather | bytes 557056 | tf_op jit(solution)/shard_map/all_gather | solution.py:133
  242.0 17.6 %all-gather.14 = bf16[1,2048]{1,0:T(2,128)(2,1)S(1)} all-gather(bf16[1,128]{1,0:T(2,128)(2,1)S(1)} %get-tuple-element.162), channel_id=16, replica_groups=mesh['rep'=2,'shard'=16] {'shard'}, dimensions={1}, use_global_device_ids=true | all-gather | bytes 4352 | tf_op jit(solution)/shard_map/all_gather | solution.py:141
  270.8 2.6 copy.312
  283.8 7.4 fusion.20
  291.1 3.2 fusion.57
  304.9 2.6 copy.324
  308.8 2.6 copy.325
  311.5 2.3 reshape.792
  313.7 2.6 copy.328
  334.1 7.0 fusion.23
  341.1 3.9 fusion.150
  349.5 4.6 multiply_reduce_fusion.2
  354.7 3.2 fusion.60
  357.8 2.3 reshape.774
  360.1 5.4 fusion.130
  377.4 2.3 reshape.796
  379.7 2.6 copy.337
  382.3 2.7 multiply_reduce_fusion.1
  394.0 2.2 copy.347
  398.3 2.2 copy.341
  404.1 2.7 convolution_add_fusion.3
  414.5 4.8 multiply_reduce_fusion.3
  419.3 4.3 fusion.129
  423.6 2.7 convert_reduce_fusion.6
  426.4 3.9 fusion.151
  432.2 3.7 multiply_reduce_fusion.4
  435.9 3.4 fusion.128
  439.3 2.7 convert_reduce_fusion.4
  443.2 2.3 reshape.798
  447.4 3.4 multiply_reduce_fusion
  451.1 3.0 convert_reduce_fusion.1
  488.4 31.7 %all-reduce.2 = (bf16[2048]{0:T(1024)(128)(2,1)S(1)}, bf16[2048]{0:T(1024)(128)(2,1)S(1)}) all-reduce(bf16[2048]{0:T(1024)(128)(2,1)S(1)} %copy-done.105, bf16[2048]{0:T(1024)(128)(2,1)S(1)} %copy-done.106), channel_id=33, replica_groups=mesh['rep'=2,'shard'=16] {'shard'}, use_global_device_ids=true, to_apply=%region_63.64.clone | all-reduce | flops 4096 | bytes 16384
  522.2 3.1 multiply_reduce_fusion.5
  525.3 3.4 fusion.127
  532.0 57.7 %psum.78 = f32[2,169,16]{1,2,0:T(8,128)S(1)} all-reduce(f32[2,169,16]{1,2,0:T(8,128)S(1)} %pad_maximum_fusion.10), channel_id=1, replica_groups=mesh['rep'=2,'shard'=16] {'shard'}, use_global_device_ids=true, to_apply=%region_67.68 | all-reduce | flops 5408 | bytes 43264 | tf_op jit(solution)/shard_map/psum | solution.py:342
  590.8 9.0 psum.79
  602.9 23.8 %reduce-scatter.27.cloned.1.call-done = bf16[32,1536]{1,0:T(8,128)(2,1)} async-done(((bf16[512,1536]{1,0:T(8,128)(2,1)}), bf16[32,1536]{1,0:T(8,128)(2,1)}) %reduce-scatter.27.cloned.1.call-update) | async-done | bytes 98320 | tf_op jit(solution)/shard_map/reduce_scatter | solution.py:301
  626.7 62.5 %reduce-scatter.29.cloned.1.call-done = bf16[32,1536]{1,0:T(8,128)(2,1)} async-done(((bf16[512,1536]{1,0:T(8,128)(2,1)}), bf16[32,1536]{1,0:T(8,128)(2,1)}) %reduce-scatter.29.cloned.1.call-update) | async-done | bytes 98320 | tf_op jit(solution)/shard_map/reduce_scatter | solution.py:301
  690.9 62.7 %reduce-scatter.37.cloned.1.call-done = bf16[32,2048]{1,0:T(8,128)(2,1)} async-done(((bf16[512,2048]{1,0:T(8,128)(2,1)}), bf16[32,2048]{1,0:T(8,128)(2,1)}) %reduce-scatter.37.cloned.1.call-update) | async-done | bytes 131088 | tf_op jit(solution)/shard_map/reduce_scatter | solution.py:318
  753.6 64.6 %reduce-scatter.35.cloned.1.call-done = bf16[32,2048]{1,0:T(8,128)(2,1)} async-done(((bf16[512,2048]{1,0:T(8,128)(2,1)}), bf16[32,2048]{1,0:T(8,128)(2,1)}) %reduce-scatter.35.cloned.1.call-update) | async-done | bytes 131088 | tf_op jit(solution)/shard_map/reduce_scatter | solution.py:318
  819.9 62.7 %reduce-scatter.39.cloned.1.call-done = bf16[128,512]{1,0:T(8,128)(2,1)} async-done(((bf16[2048,512]{1,0:T(8,128)(2,1)}), bf16[128,512]{1,0:T(8,128)(2,1)}) %reduce-scatter.39.cloned.1.call-update) | async-done | bytes 131088 | tf_op jit(solution)/shard_map/reduce_scatter | solution.py:321
  882.6 64.7 %reduce-scatter.41.cloned.1.call-done = bf16[128,512]{1,0:T(8,128)(2,1)} async-done(((bf16[2048,512]{1,0:T(8,128)(2,1)}), bf16[128,512]{1,0:T(8,128)(2,1)}) %reduce-scatter.41.cloned.1.call-update) | async-done | bytes 131088 | tf_op jit(solution)/shard_map/reduce_scatter | solution.py:321
  950.2 54.4 %reduce-scatter.47.cloned.1.call-done = bf16[32,2]{1,0:T(8,128)(2,1)} async-done(((bf16[512,2]{1,0:T(8,128)(2,1)}), bf16[32,2]{1,0:T(8,128)(2,1)}) %reduce-scatter.47.cloned.1.call-update) | async-done | bytes 144
  1005.4 56.7 %reduce-scatter.49.cloned.1.call-done = bf16[32,2]{1,0:T(8,128)(2,1)} async-done(((bf16[512,2]{1,0:T(8,128)(2,1)}), bf16[32,2]{1,0:T(8,128)(2,1)}) %reduce-scatter.49.cloned.1.call-update) | async-done | bytes 144
  1062.9 56.7 %reduce-scatter.43.cloned.1.call-done = bf16[32,2]{1,0:T(8,128)(2,1)} async-done(((bf16[512,2]{1,0:T(8,128)(2,1)}), bf16[32,2]{1,0:T(8,128)(2,1)}) %reduce-scatter.43.cloned.1.call-update) | async-done | bytes 144
  1120.3 57.3 %reduce-scatter.45.cloned.1.call-done = bf16[32,2]{1,0:T(8,128)(2,1)} async-done(((bf16[512,2]{1,0:T(8,128)(2,1)}), bf16[32,2]{1,0:T(8,128)(2,1)}) %reduce-scatter.45.cloned.1.call-update) | async-done | bytes 144
  1178.4 56.8 %reduce-scatter.51.cloned.1.call-done = bf16[32,4]{1,0:T(8,128)(2,1)} async-done(((bf16[512,4]{1,0:T(8,128)(2,1)}), bf16[32,4]{1,0:T(8,128)(2,1)}) %reduce-scatter.51.cloned.1.call-update) | async-done | bytes 272
  1235.9 56.7 %reduce-scatter.53.cloned.1.call-done = bf16[32,4]{1,0:T(8,128)(2,1)} async-done(((bf16[512,4]{1,0:T(8,128)(2,1)}), bf16[32,4]{1,0:T(8,128)(2,1)}) %reduce-scatter.53.cloned.1.call-update) | async-done | bytes 272
  1293.4 5.0 all-reduce.3
  1300.7 28.9 %all-reduce.7.cloned.1.call-done = (bf16[2,32,1536]{2,1,0:T(8,128)(2,1)}, bf16[2,32,512]{2,1,0:T(8,128)(2,1)}, bf16[2,32,2048]{2,1,0:T(8,128)(2,1)}, bf16[2,128,512]{2,1,0:T(8,128)(2,1)}) async-done(((bf16[2,32,1536]{2,1,0:T(8,128)(2,1)}, bf16[2,32,512]{2,1,0:T(8,128)(2,1)}, bf16[2,32,2048]{2,1,0:T(8,128)(2,1)}, bf16[2,128,512]{2,1,0:T(8,128)(2,1)}), (bf16[2,32,1536]{2,1,0:T(8,128)(2,1)}, ...) | async-done | bytes 786448 | tf_op jit(solution)/shard_map/psum | solution.py:71
  (513 shorter events, 172.4 us)
Async XLA Ops:
  7.2 7.3 copy-start.111
  7.2 253.7 %all-gather.23.cloned.1.call-start = ((), (), s32[]{:S(2)}) async-start(), calls=%async_computation.22 | async-start | bytes 1671168 | tf_op jit(solution)/shard_map/all_gather | solution.py:132
  8.9 6.8 copy-start.2
  8.9 274.9 %all-gather.25.cloned.1.call-start = ((), (), s32[]{:S(2)}) async-start(), calls=%async_computation.23 | async-start | bytes 2228224 | tf_op jit(solution)/shard_map/all_gather | solution.py:139
  10.7 6.7 copy-start.109
  10.7 280.4 %all-gather.27.cloned.1.call-start = ((), (), s32[]{:S(2)}) async-start(), calls=%async_computation.24 | async-start | bytes 2228224 | tf_op jit(solution)/shard_map/all_gather | solution.py:140
  12.4 288.3 %all-gather.29.cloned.1.call-start = ((), (), s32[]{:S(2)}) async-start(), calls=%async_computation.25 | async-start | bytes 1671168 | tf_op jit(solution)/shard_map/all_gather | solution.py:132
  13.0 321.1 %all-gather.31.cloned.1.call-start = ((), (), s32[]{:S(2)}) async-start(), calls=%async_computation.26 | async-start | bytes 2228224 | tf_op jit(solution)/shard_map/all_gather | solution.py:139
  13.6 327.5 %all-gather.33.cloned.1.call-start = ((), (), s32[]{:S(2)}) async-start(), calls=%async_computation.27 | async-start | bytes 2228224 | tf_op jit(solution)/shard_map/all_gather | solution.py:140
  14.2 587.3 %reduce-scatter.33.cloned.1.call-start = ((), (), s32[]{:S(2)}) async-start(), calls=%async_computation.17 | async-start | bytes 557056 | tf_op jit(solution)/shard_map/reduce_scatter | solution.py:304
  14.3 30.3 %copy-start.110 = (bf16[2,2,32]{2,1,0:T(2,128)(2,1)S(1)}, bf16[2,2,32]{2,1,0:T(2,128)(2,1)}, u32[]{:S(2)}) copy-start(bf16[2,2,32]{2,1,0:T(2,128)(2,1)} %param.20) | copy-start | bytes 772
  16.3 50.0 %copy-start.60 = (f32[14,14]{1,0:T(8,128)}, f32[14,14]{1,0:T(8,128)S(1)}, u32[]{:S(2)}) copy-start(f32[14,14]{1,0:T(8,128)S(1)} %broadcast_multiply_fusion.3) | copy-start | bytes 2356
  17.3 50.8 %copy-start.70 = (f32[14,14]{1,0:T(8,128)}, f32[14,14]{1,0:T(8,128)S(1)}, u32[]{:S(2)}) copy-start(f32[14,14]{1,0:T(8,128)S(1)} %multiply_reduce_fusion.13) | copy-start | bytes 2356
  17.4 49.0 %copy-start.68 = (f32[14,14]{1,0:T(8,128)}, f32[14,14]{1,0:T(8,128)S(1)}, u32[]{:S(2)}) copy-start(f32[14,14]{1,0:T(8,128)S(1)} %fusion.110) | copy-start | bytes 2356
  44.6 21.7 %copy-start.78 = (f32[512]{0:T(512)}, f32[512]{0:T(512)S(1)}, u32[]{:S(2)}) copy-start(f32[512]{0:T(512)S(1)} %get-tuple-element.102) | copy-start | bytes 6148
  44.6 237.6 %copy-start.80 = (f32[512]{0:T(512)}, f32[512]{0:T(512)S(1)}, u32[]{:S(2)}) copy-start(f32[512]{0:T(512)S(1)} %get-tuple-element.101) | copy-start | bytes 6148
  44.7 23.6 %copy-start.107 = (bf16[2,4,32]{2,1,0:T(4,128)(2,1)S(1)}, bf16[2,4,32]{2,1,0:T(4,128)(2,1)}, u32[]{:S(2)}) copy-start(bf16[2,4,32]{2,1,0:T(4,128)(2,1)} %param.21) | copy-start | bytes 1540
  68.2 192.7 %copy-start.39 = (bf16[196,512]{1,0:T(8,128)(2,1)}, bf16[196,512]{1,0:T(8,128)(2,1)S(1)}, u32[]{:S(2)}) copy-start(bf16[196,512]{1,0:T(8,128)(2,1)S(1)} %reshape_reshape.24) | copy-start | bytes 602116
  68.4 27.7 %copy-start.77 = (bf16[2,32,512]{2,1,0:T(8,128)(2,1)S(1)}, bf16[2,32,512]{2,1,0:T(8,128)(2,1)}, u32[]{:S(2)}) copy-start(bf16[2,32,512]{2,1,0:T(8,128)(2,1)} %param.16) | copy-start | bytes 196612
  88.9 26.7 %copy-start.108 = (bf16[2,128]{1,0:T(2,128)(2,1)S(1)}, bf16[2,128]{1,0:T(2,128)(2,1)}, u32[]{:S(2)}) copy-start(bf16[2,128]{1,0:T(2,128)(2,1)} %param.22) | copy-start | bytes 1540
  115.6 161.9 %copy-start.4 = (bf16[1,512,512]{2,1,0:T(8,128)(2,1)}, bf16[1,512,512]{2,1,0:T(8,128)(2,1)S(1)}, u32[]{:S(2)}) copy-start(bf16[1,512,512]{2,1,0:T(8,128)(2,1)S(1)} %all-gather.4) | copy-start | bytes 1572868
  156.1 141.9 %copy-start.82 = (f32[512]{0:T(512)}, f32[512]{0:T(512)S(1)}, u32[]{:S(2)}) copy-start(f32[512]{0:T(512)S(1)} %get-tuple-element.94) | copy-start | bytes 6148
  179.2 40.3 %copy-start.95 = (s32[1,14,14]{2,0,1:T(1,128)S(1)}, s32[1,14,14]{2,0,1:T(1,128)}, u32[]{:S(2)}) copy-start(s32[1,14,14]{2,0,1:T(1,128)} %param.14) | copy-start | bytes 2356
  210.9 49.2 %copy-start.25 = (bf16[1,14,14,512]{3,2,1,0:T(8,128)(2,1)S(1)}, bf16[1,14,14,512]{3,2,1,0:T(8,128)(2,1)}, u32[]{:S(2)}) copy-start(bf16[1,14,14,512]{3,2,1,0:T(8,128)(2,1)} %param.13) | copy-start | bytes 602116
  269.4 5.5 copy-start.37
  283.7 7.4 copy-start.42
  308.8 7.5 copy-start.31
  322.9 5.7 copy-start.21
  354.7 5.4 copy-start.85
  410.4 8.9 copy-start.75
  432.2 7.2 copy-start.35
  442.2 8.6 copy-start.29
  450.8 150.7 %reduce-scatter.31.cloned.1.call-start = ((), (), s32[]{:S(2)}) async-start(), calls=%async_computation.16 | async-start | bytes 557056 | tf_op jit(solution)/shard_map/reduce_scatter | solution.py:304
  454.7 5.4 copy-start.38
  460.0 166.7 %reduce-scatter.27.cloned.1.call-start = ((), (), s32[]{:S(2)}) async-start(), calls=%async_computation.14 | async-start | bytes 1671168 | tf_op jit(solution)/shard_map/reduce_scatter | solution.py:301
  466.1 223.2 %reduce-scatter.29.cloned.1.call-start = ((), (), s32[]{:S(2)}) async-start(), calls=%async_computation.15 | async-start | bytes 1671168 | tf_op jit(solution)/shard_map/reduce_scatter | solution.py:301
  468.0 285.6 %reduce-scatter.37.cloned.1.call-start = ((), (), s32[]{:S(2)}) async-start(), calls=%async_computation.19 | async-start | bytes 2228224 | tf_op jit(solution)/shard_map/reduce_scatter | solution.py:318
  471.2 346.9 %reduce-scatter.35.cloned.1.call-start = ((), (), s32[]{:S(2)}) async-start(), calls=%async_computation.18 | async-start | bytes 2228224 | tf_op jit(solution)/shard_map/reduce_scatter | solution.py:318
  474.5 408.1 %reduce-scatter.39.cloned.1.call-start = ((), (), s32[]{:S(2)}) async-start(), calls=%async_computation.20 | async-start | bytes 2228224 | tf_op jit(solution)/shard_map/reduce_scatter | solution.py:321
  477.8 469.4 %reduce-scatter.41.cloned.1.call-start = ((), (), s32[]{:S(2)}) async-start(), calls=%async_computation.21 | async-start | bytes 2228224 | tf_op jit(solution)/shard_map/reduce_scatter | solution.py:321
  481.2 523.4 %reduce-scatter.47.cloned.1.call-start = ((), (), s32[]{:S(2)}) async-start(), calls=%async_computation.30 | async-start | bytes 139264
  486.9 33.2 %copy-start.88 = (s32[2401]{0:T(1024)S(1)}, s32[2401]{0:T(1024)}, u32[]{:S(2)}) copy-start(s32[2401]{0:T(1024)} %copy-done.87) | copy-start | bytes 28816
  487.0 34.2 %copy-start.63 = (f32[16,2401]{1,0:T(8,128)S(1)}, f32[16,2401]{1,0:T(8,128)}, u32[]{:S(2)}) copy-start(f32[16,2401]{1,0:T(8,128)} %reshape.716) | copy-start | bytes 460996
  487.9 34.3 %copy-start.3 = (bf16[1,14,14,512]{3,2,1,0:T(8,128)(2,1)S(1)}, bf16[1,14,14,512]{3,2,1,0:T(8,128)(2,1)}, u32[]{:S(2)}) copy-start(bf16[1,14,14,512]{3,2,1,0:T(8,128)(2,1)} %param.12) | copy-start | bytes 602116
  487.9 34.3 %copy-start.61 = (f32[14,14]{1,0:T(8,128)S(1)}, f32[14,14]{1,0:T(8,128)}, u32[]{:S(2)}) copy-start(f32[14,14]{1,0:T(8,128)} %copy-done.60) | copy-start | bytes 2356
  487.9 34.3 %copy-start.69 = (f32[14,14]{1,0:T(8,128)S(1)}, f32[14,14]{1,0:T(8,128)}, u32[]{:S(2)}) copy-start(f32[14,14]{1,0:T(8,128)} %copy-done.68) | copy-start | bytes 2356
  487.9 34.3 %copy-start.79 = (f32[512]{0:T(512)S(1)}, f32[512]{0:T(512)}, u32[]{:S(2)}) copy-start(f32[512]{0:T(512)} %copy-done.78) | copy-start | bytes 6148
  488.0 37.3 %copy-start.71 = (f32[14,14]{1,0:T(8,128)S(1)}, f32[14,14]{1,0:T(8,128)}, u32[]{:S(2)}) copy-start(f32[14,14]{1,0:T(8,128)} %copy-done.70) | copy-start | bytes 2356
  520.2 9.6 copy-start.103
  521.1 9.6 copy-start.101
  521.1 9.6 copy-start.98
  521.1 9.9 copy-start.102
  521.1 9.9 copy-start.100
  522.1 68.4 %copy-start.96 = (bf16[512]{0:T(512)(128)(2,1)S(1)}, bf16[512]{0:T(512)(128)(2,1)}, u32[]{:S(2)}) copy-start(bf16[512]{0:T(512)(128)(2,1)} %get-tuple-element.119) | copy-start | bytes 3076
  522.1 68.4 %copy-start.97 = (bf16[512]{0:T(512)(128)(2,1)S(1)}, bf16[512]{0:T(512)(128)(2,1)}, u32[]{:S(2)}) copy-start(bf16[512]{0:T(512)(128)(2,1)} %get-tuple-element.145) | copy-start | bytes 3076
  522.1 68.4 %copy-start.86 = (bf16[16,32]{1,0:T(8,128)(2,1)S(1)}, bf16[16,32]{1,0:T(8,128)(2,1)}, u32[]{:S(2)}) copy-start(bf16[16,32]{1,0:T(8,128)(2,1)} %get-tuple-element.182) | copy-start | bytes 3076
  522.2 78.5 %copy-start.33 = (bf16[1,14,14,512]{3,0,2,1:T(2,128)(2,1)S(1)}, bf16[1,14,14,512]{3,0,2,1:T(2,128)(2,1)}, u32[]{:S(2)}) copy-start(bf16[1,14,14,512]{3,0,2,1:T(2,128)(2,1)} %get-tuple-element.147) | copy-start | bytes 602116
  528.8 533.3 %reduce-scatter.49.cloned.1.call-start = ((), (), s32[]{:S(2)}) async-start(), calls=%async_computation.31 | async-start | bytes 139264
  529.8 589.8 %reduce-scatter.43.cloned.1.call-start = ((), (), s32[]{:S(2)}) async-start(), calls=%async_computation.28 | async-start | bytes 139264
  530.8 646.8 %reduce-scatter.45.cloned.1.call-start = ((), (), s32[]{:S(2)}) async-start(), calls=%async_computation.29 | async-start | bytes 139264
  531.9 703.3 %reduce-scatter.51.cloned.1.call-start = ((), (), s32[]{:S(2)}) async-start(), calls=%async_computation.32 | async-start | bytes 139264
  590.7 701.9 %reduce-scatter.53.cloned.1.call-start = ((), (), s32[]{:S(2)}) async-start(), calls=%async_computation.33 | async-start | bytes 139264
  599.8 349.1 %copy-start.34 = (f32[1,14,14,512]{3,0,2,1:T(1,128)S(1)}, f32[1,14,14,512]{3,0,2,1:T(1,128)}, u32[]{:S(2)}) copy-start(f32[1,14,14,512]{3,0,2,1:T(1,128)} %get-tuple-element.127) | copy-start | bytes 1204228
  601.4 728.2 %all-reduce.7.cloned.1.call-start = ((), (), s32[]{:S(2)}) async-start(), calls=%async_computation.34 | async-start | bytes 1572864 | tf_op jit(solution)/shard_map/psum | solution.py:71
  (71 other events, 166.4 us)
Sparse Core Ops, SparseCore 0:
  10.9 42.6 all-gather.22
  56.3 40.3 all-gather.24
  99.4 40.4 all-gather.26
  142.1 38.7 all-gather.28
  183.4 40.6 all-gather.30
  226.7 40.3 all-gather.32
  450.9 54.1 reduce-scatter.32
  509.6 54.8 reduce-scatter.30
  568.2 58.5 reduce-scatter.26
  630.7 58.5 reduce-scatter.28
  693.0 60.5 reduce-scatter.36
  757.6 60.5 reduce-scatter.34
  821.9 60.5 reduce-scatter.38
  886.6 60.5 reduce-scatter.40
  950.5 54.0 reduce-scatter.46
  1008.0 54.0 reduce-scatter.48
  1065.4 54.0 reduce-scatter.42
  1123.4 54.1 reduce-scatter.44
  1181.0 54.0 reduce-scatter.50
  1238.5 54.1 reduce-scatter.52
  1295.7 33.9 all-reduce.6
